TPU v7x, 512 devices: a whole 4x4x16 slice. The times are simulated.
512 devices in a mesh: dp: 32 (over z, y_lo), fsdp: 16 (over x, y_hi, core).
Axes of the slice: x: 4, y: 4 (y_hi: 2, y_lo: 2; y = y_hi * 2 + y_lo), z: 16, core: 2. Of those that a mesh axis runs over, the one named last changes fastest.
Arguments:
- tokens: bfloat16 [65536, 1024], P(('dp', 'fsdp')), may hold values from -6 to 6
- cotangent: bfloat16 [65536, 1024], P(('dp', 'fsdp')), may hold values from -6 to 6
- routes: int32 [65536, 1], P(('dp', 'fsdp')), may hold values from 0 to 32; in each aligned block of 128 rows (0 to 127, 128 to 255, ...) at most 4 rows name the same one
- norm_gain_vector: float32 [1024], replicated, may hold values from 0.25 to 1.75
- up_weight: bfloat16 [1024, 4096], P(None, 'fsdp'), may hold values from -0.1875 to 0.1875
- up_bias: float32 [4096], P('fsdp'), may hold values from -4 to 4
- down_weight: bfloat16 [4096, 1024], P('fsdp'), may hold values from -0.09375 to 0.09375
Outputs:
- input_grad: bfloat16 [65536, 1024], P(('dp', 'fsdp'))
- up_grad: float32 [1024, 4096], P(None, 'fsdp')
- bias_grad: float32 [4096], P('fsdp')
- down_grad: float32 [4096, 1024], P('fsdp')
- gain_grad: float32 [1024], replicated
Inputs may be any that keep to these rules, and one draw needn't show every extreme that they name: `routes`: among the 128 slots of one device no value below 32 appears more than 4 times; the value 32 marks a padding slot.
All inputs are finite; a program needn't handle non-finite values.
Results may differ from a plain program's by a relative error of at most 0.024.
Values may be sent and summed in bfloat16 or wider, within the bound.
A program may use at most 128 MiB of HBM per device.

v0:
```python
import jax
import jax.numpy as jnp
from jax import lax
from jax.sharding import Mesh
from jax.sharding import PartitionSpec as P

DP = ("dp_0", "dp_1")
FSDP = ("fsdp_0", "fsdp_1", "fsdp_2")
ROWS_AXES = ("fsdp_0", "fsdp_1")
DP_FSDP = ("dp_0", "dp_1", "fsdp_0", "fsdp_1", "fsdp_2")
root_two_pi = 0.7978845608
cubic = 0.044715


def side_by_side(arrays, axis, split_dim, concat_dim, along):
    both = jnp.concatenate(arrays, axis=along)
    filled, at, finished = (
        lax.all_to_all(both, axis, split_axis=split_dim, concat_axis=concat_dim, tiled=True),
        0,
        [],
    )
    for a in arrays:
        finished.append(lax.slice_in_dim(filled, at, at + a.shape[along], axis=along))
        at += a.shape[along]
    return tuple(finished)


def gelu_pair(pre):
    inner = root_two_pi * (pre + cubic * pre * pre * pre)
    tangent = jnp.tanh(inner)
    act = 0.5 * pre * (1.0 + tangent)
    slope = 0.5 * (1.0 + tangent) + 0.5 * pre * (1.0 - tangent * tangent) * root_two_pi * (
        1.0 + 3.0 * cubic * pre * pre
    )
    return (act, slope)


def apply_layer_norm(values):
    row_average = jnp.mean(values, axis=1, keepdims=True)
    centered = values - row_average
    variance = jnp.mean(centered * centered, axis=1, keepdims=True)
    inverse_std = 1.0 / jnp.sqrt(variance + 1e-05)
    return (centered * inverse_std, inverse_std)


def shards(tokens, cotangent, routes, norm_gain_vector, up_weight, up_bias, down_weight):
    particle_slot_count = tokens.shape[0]
    dp_size = lax.axis_size(DP)
    capacity = particle_slot_count // dp_size
    up_weight = lax.all_gather(up_weight, "fsdp_2", axis=1, tiled=True)
    down_weight = lax.all_gather(down_weight, "fsdp_2", axis=0, tiled=True)
    up_bias = lax.all_gather(up_bias, "fsdp_2", axis=0, tiled=True)
    target = routes[:, 0]
    matches = (target[:, None] == jnp.arange(dp_size + 1, dtype=jnp.int32)[None, :]).astype(
        jnp.int32
    )
    earlier = jnp.cumsum(matches, axis=0) - matches
    ranked = jnp.sum(earlier * matches, axis=1)
    slot_index = jnp.where(target < dp_size, target * capacity + ranked, -1)
    placing = (
        slot_index[None, :] == jnp.arange(particle_slot_count, dtype=jnp.int32)[:, None]
    ).astype(jnp.bfloat16)
    send_in = jnp.dot(placing, tokens, preferred_element_type=jnp.float32).astype(jnp.bfloat16)
    send_cot = jnp.dot(placing, cotangent, preferred_element_type=jnp.float32).astype(jnp.bfloat16)
    packed_in, packed_cot = side_by_side((send_in, send_cot), DP, 0, 0, 1)
    local_standardized, own_inverse = apply_layer_norm(packed_in.astype(jnp.float32))
    normed_local = (local_standardized * norm_gain_vector).astype(jnp.bfloat16)
    all_cot = lax.all_gather(packed_cot, ROWS_AXES, axis=0, tiled=True)
    gathered_normed_rows = lax.all_gather(normed_local, ROWS_AXES, axis=0, tiled=True)
    pre = jnp.dot(gathered_normed_rows, up_weight, preferred_element_type=jnp.float32) + up_bias
    act_full, slope = gelu_pair(pre)
    act = act_full.astype(jnp.bfloat16)
    act_grad = jnp.einsum("rd,kd->rk", all_cot, down_weight, preferred_element_type=jnp.float32)
    pre_grad = (act_grad * slope).astype(jnp.bfloat16)
    down_part = jnp.einsum("rk,rd->kd", act, all_cot, preferred_element_type=jnp.float32)
    up_part = jnp.einsum(
        "rk,rd->kd", pre_grad, gathered_normed_rows, preferred_element_type=jnp.float32
    )
    bias_part = jnp.sum(pre_grad.astype(jnp.float32), axis=0)
    partial_gain_grad = (
        jnp.sum(up_part * up_weight.T.astype(jnp.float32), axis=0) / norm_gain_vector
    )
    parts = jnp.concatenate([up_part, down_part], axis=1).astype(jnp.bfloat16)
    mine = lax.psum_scatter(parts, "fsdp_2", scatter_dimension=0, tiled=True)
    mine = lax.psum_scatter(mine, DP, scatter_dimension=0, tiled=True)
    whole = lax.all_gather(mine, DP, axis=0, tiled=True).astype(jnp.float32)
    d = up_weight.shape[0]
    up_grad = whole[:, :d].T
    down_grad = whole[:, d:]
    normed_rows_gradient = lax.psum_scatter(
        jnp.einsum("rk,dk->rd", pre_grad, up_weight, preferred_element_type=jnp.float32).astype(
            jnp.bfloat16
        ),
        ROWS_AXES,
        scatter_dimension=0,
        tiled=True,
    ).astype(jnp.float32)
    index = lax.axis_index(FSDP)
    k = bias_part.shape[0] // 2
    wide = jnp.zeros((8, 2 * k), jnp.float32)
    wide = lax.dynamic_update_slice(wide, bias_part[None], (index // 2, 0))
    small = lax.psum(jnp.concatenate([partial_gain_grad, wide.reshape(-1)]), DP_FSDP)
    gain_grad = small[:d]
    bias_grad = lax.dynamic_slice(small[d:], (index * k,), (k,))
    scaled_values = normed_rows_gradient * norm_gain_vector
    final_result = packed_cot.astype(jnp.float32) + own_inverse * (
        scaled_values
        - jnp.mean(scaled_values, axis=1, keepdims=True)
        - local_standardized * jnp.mean(scaled_values * local_standardized, axis=1, keepdims=True)
    )
    return (final_result.astype(jnp.bfloat16), up_grad, bias_grad, down_grad, gain_grad)


def solution(mesh):
    finer = Mesh(
        mesh.devices.reshape(16, 2, 4, 2, 2), ("dp_0", "dp_1", "fsdp_0", "fsdp_1", "fsdp_2")
    )
    return jax.shard_map(
        shards,
        mesh=finer,
        in_specs=(
            P(DP_FSDP, None),
            P(DP_FSDP, None),
            P(DP_FSDP, None),
            P(),
            P(None, FSDP),
            P(FSDP),
            P(FSDP, None),
        ),
        out_specs=(P(DP_FSDP, None), P(None, FSDP), P(FSDP), P(FSDP, None), P()),
        check_vma=False,
    )
```

profile of v0, /device:TPU:2, one launch (start us, length us, event | category | flops | bytes accessed | tf_op | source)
XLA Modules:
  0.0 631.0 jit_solution(15258363506738329338)
XLA Ops:
  7.2 0.8 fusion.26
  8.1 0.8 select_reduce_fusion
  9.0 0.7 compare_select_fusion
  9.9 1.2 convolution_convert_fusion.3
  11.1 1.0 all_to_all.8
  12.1 16.6 %all-to-all-start = ((bf16[32,4,2048]{2,1,0:T(4,128)(2,1)}), bf16[32,4,2048]{2,1,0:T(4,128)(2,1)S(1)}, u32[]{:S(2)}, u32[]{:S(2)}) async-start(bf16[32,4,2048]{2,1,0:T(4,128)(2,1)} %all_to_all.8), calls=%async_computation | async-start | bytes 1048576 | tf_op jit(solution)/shard_map/all_to_all | solution.py:18
  28.8 1.0 copy.14
  29.9 31.9 %all-to-all-done = bf16[32,4,2048]{2,1,0:T(4,128)(2,1)S(1)} async-done(((bf16[32,4,2048]{2,1,0:T(4,128)(2,1)}), bf16[32,4,2048]{2,1,0:T(4,128)(2,1)S(1)}, u32[]{:S(2)}, u32[]{:S(2)}) %all-to-all-start) | async-done | bytes 524320 | tf_op jit(solution)/shard_map/all_to_all | solution.py:18
  62.2 0.9 fusion.18
  63.2 0.7 slice.24
  64.0 0.5 all-gather.9.cloned.1.call-update
  64.6 1.8 all-gather
  66.4 61.5 %all-gather.11.cloned.1.call-done = bf16[1024,1024]{1,0:T(8,128)(2,1)} async-done(((bf16[128,1024]{1,0:T(8,128)(2,1)}), bf16[1024,1024]{1,0:T(8,128)(2,1)}) %all-gather.11.cloned.1.call-update) | async-done | bytes 2097168 | tf_op jit(solution)/shard_map/all_gather | solution.py:69
  127.9 4.4 fusion.33
  132.4 68.8 %all-gather.7.cloned.1.call-done = bf16[1024,1024]{1,0:T(8,128)(2,1)} async-done(((bf16[128,1024]{1,0:T(8,128)(2,1)}), bf16[1024,1024]{1,0:T(8,128)(2,1)}) %all-gather.7.cloned.1.call-update) | async-done | bytes 2097168 | tf_op jit(solution)/shard_map/all_gather | solution.py:68
  201.1 3.6 convolution_convert_fusion.1
  204.8 17.0 %all-gather.9.cloned.1.call-done = bf16[512,1024]{1,0:T(8,128)(2,1)} async-done(((bf16[256,1024]{1,0:T(8,128)(2,1)}), bf16[512,1024]{1,0:T(8,128)(2,1)}) %all-gather.9.cloned.1.call-update) | async-done | bytes 1048592 | tf_op jit(solution)/shard_map/all_gather | solution.py:51
  221.8 5.1 convert_reduce_fusion
  226.9 1.3 fusion.7
  228.2 1.5 pad_maximum_fusion
  229.8 21.8 %reduce-scatter.6.cloned.1.call-done = bf16[256,2048]{1,0:T(8,128)(2,1)} async-done(((bf16[512,2048]{1,0:T(8,128)(2,1)}), bf16[256,2048]{1,0:T(8,128)(2,1)}) %reduce-scatter.6.cloned.1.call-update) | async-done | bytes 1048592 | tf_op jit(solution)/shard_map/reduce_scatter | solution.py:84
  251.6 2.6 convolution_convert_fusion
  254.3 139.2 %reduce-scatter.8.cloned.1.call-done = bf16[8,2048]{1,0:T(8,128)(2,1)} async-done(((bf16[256,2048]{1,0:T(8,128)(2,1)}), bf16[8,2048]{1,0:T(8,128)(2,1)}) %reduce-scatter.8.cloned.1.call-update) | async-done | bytes 32784 | tf_op jit(solution)/shard_map/reduce_scatter | solution.py:85
  393.7 100.6 %psum.7 = f32[5120]{0:T(1024)S(1)} all-reduce(f32[5120]{0:T(1024)S(1)} %pad_maximum_fusion.2), channel_id=1, replica_groups=mesh['dp_0'=16,'dp_1'=2,'fsdp_0'=4,'fsdp_1'=2,'fsdp_2'=2] {'dp_0','dp_1'..., use_global_device_ids=true, to_apply=%region_11.12 | all-reduce | flops 5120 | bytes 40960 | tf_op jit(solution)/shard_map/psum | solution.py:102
  494.2 0.6 slice.29
  494.8 0.6 dynamic_slice.3
  495.5 1.2 fusion.25
  496.7 1.9 fusion.23
  498.6 121.5 %all-gather.15.cloned.1.call-done = bf16[256,2048]{1,0:T(8,128)(2,1)} async-done(((bf16[8,2048]{1,0:T(8,128)(2,1)}), bf16[256,2048]{1,0:T(8,128)(2,1)}) %all-gather.15.cloned.1.call-update) | async-done | bytes 1048592 | tf_op jit(solution)/shard_map/all_gather | solution.py:86
  620.1 1.5 convert_element_type.58
  621.7 1.3 copy.15
  623.0 1.1 slice.28
  (51 shorter events, 1.6 us)
Async XLA Ops:
  7.2 2.5 copy-start
  9.6 19.1 %copy-start.2 = (bf16[1024,256]{1,0:T(8,128)(2,1)S(1)}, bf16[1024,256]{1,0:T(8,128)(2,1)}, u32[]{:S(2)}) copy-start(bf16[1024,256]{1,0:T(8,128)(2,1)} %param.11) | copy-start | bytes 1572868
  12.1 50.1 %copy-start.3 = (f32[1024]{0:T(1024)S(1)}, f32[1024]{0:T(1024)}, u32[]{:S(2)}) copy-start(f32[1024]{0:T(1024)} %param.10) | copy-start | bytes 12292
  12.1 49.7 %all-to-all-start = ((bf16[32,4,2048]{2,1,0:T(4,128)(2,1)}), bf16[32,4,2048]{2,1,0:T(4,128)(2,1)S(1)}, u32[]{:S(2)}, u32[]{:S(2)}) async-start(bf16[32,4,2048]{2,1,0:T(4,128)(2,1)} %all_to_all.8), calls=%async_computation | async-start | bytes 1048576 | tf_op jit(solution)/shard_map/all_to_all | solution.py:18
  28.7 37.7 %all-gather.13.cloned.1.call-start = ((), (), s32[]{:S(2)}) async-start(), calls=%async_computation.7 | async-start | bytes 1572864 | tf_op jit(solution)/shard_map/all_gather | solution.py:50
  29.8 34.8 %copy-start.4 = (f32[256]{0:T(256)S(1)}, f32[256]{0:T(256)}, u32[]{:S(2)}) copy-start(f32[256]{0:T(256)} %param.12) | copy-start | bytes 3076
  29.8 98.1 %all-gather.11.cloned.1.call-start = ((), (), s32[]{:S(2)}) async-start(), calls=%async_computation.6 | async-start | bytes 2359296 | tf_op jit(solution)/shard_map/all_gather | solution.py:69
  63.2 138.0 %all-gather.7.cloned.1.call-start = ((), (), s32[]{:S(2)}) async-start(), calls=%async_computation.4 | async-start | bytes 2359296 | tf_op jit(solution)/shard_map/all_gather | solution.py:68
  64.0 157.8 %all-gather.9.cloned.1.call-start = ((), (), s32[]{:S(2)}) async-start(), calls=%async_computation.5 | async-start | bytes 1572864 | tf_op jit(solution)/shard_map/all_gather | solution.py:51
  64.5 187.0 %reduce-scatter.6.cloned.1.call-start = ((), (), s32[]{:S(2)}) async-start(), calls=%async_computation.9 | async-start | bytes 3145728 | tf_op jit(solution)/shard_map/reduce_scatter | solution.py:84
  204.7 22.2 %copy-start.6 = (bf16[1024,512]{0,1:T(8,128)(2,1)S(1)}, bf16[1024,512]{0,1:T(8,128)(2,1)}, u32[]{:S(2)}) copy-start(bf16[1024,512]{0,1:T(8,128)(2,1)} %all-gather.13.cloned.1.call-done) | copy-start | bytes 3145732
  221.8 5.1 copy-start.5
  226.9 1.3 copy-start.7
  229.7 21.9 %copy-start.8 = (bf16[1024,512]{1,0:T(8,128)(2,1)S(1)}, bf16[1024,512]{1,0:T(8,128)(2,1)}, u32[]{:S(2)}) copy-start(bf16[1024,512]{1,0:T(8,128)(2,1)} %copy-done.7) | copy-start | bytes 3145732
  229.7 163.8 %reduce-scatter.8.cloned.1.call-start = ((), (), s32[]{:S(2)}) async-start(), calls=%async_computation.10 | async-start | bytes 1081344 | tf_op jit(solution)/shard_map/reduce_scatter | solution.py:85
  251.6 243.9 %reduce-scatter.4.cloned.1.call-start = ((), (), s32[]{:S(2)}) async-start(), calls=%async_computation.8 | async-start | bytes 2359296 | tf_op jit(solution)/shard_map/reduce_scatter | solution.py:90
  254.3 365.9 %all-gather.15.cloned.1.call-start = ((), (), s32[]{:S(2)}) async-start(), calls=%async_computation.11 | async-start | bytes 1081344 | tf_op jit(solution)/shard_map/all_gather | solution.py:86
  621.6 1.4 copy-start.1
Sparse Core Ops, SparseCore 0:
  32.2 20.3 all-gather.12
  63.3 64.5 all-gather.10
  131.7 69.3 all-gather.6
  203.1 18.6 all-gather.8
  229.9 21.6 reduce-scatter.5
  254.2 139.2 reduce-scatter.7
  398.2 89.2 reduce-scatter.3
  489.5 130.5 all-gather.14
where the time goes:
time: 631 us
  waiting for transfers between devices  462 us (73%)
  blocking collectives  102 us (16%)
  matrix products  18.4 us (3%)
  starting transfers between devices  17 us (3%)
  between operations  14.4 us (2%)
  other arithmetic  9.85 us (2%)
  local copies, waits for them, and re-layouts  6.69 us (1%)
    reduce_scatter x1, waiting for transfers between devices, shards(): mine = lax.psum_scatter(mine, DP, scatter_dimension=0, tiled=True)  139 us
    all_gather x1, waiting for transfers between devices, shards(): whole = lax.all_gather(mine, DP, axis=0, tiled=True).astype(jnp.float32)  122 us
    psum x1, blocking collectives, shards(): lax.psum(jnp.concatenate([partial_gain_grad, wide.reshape(-1)]), DP_FSDP)  101 us
    all_gather x1, waiting for transfers between devices, shards(): all_cot = lax.all_gather(packed_cot, ROWS_AXES, axis=0, tiled=True)  68.8 us
    all_gather x1, waiting for transfers between devices, shards(): lax.all_gather(normed_local, ROWS_AXES, axis=0, tiled=True)  61.5 us
    all_to_all x1, waiting for transfers between devices, side_by_side(): lax.all_to_all(both, axis, split_axis=split_dim, concat_axis=concat_dim,...  31.9 us
    reduce_scatter x1, waiting for transfers between devices, shards(): mine = lax.psum_scatter(parts, 'fsdp_2', scatter_dimension=0, tiled=True)  21.8 us
    all_gather x1, waiting for transfers between devices, shards(): down_weight = lax.all_gather(down_weight, 'fsdp_2', axis=0, tiled=True)  17 us
  transfers between devices with their start and end apart: 9, of which 7 were waited for; matrix products, arithmetic and copies ran while one was open for 3% of the time, Pallas kernels for 0%

commit v1 on v0

--- a/solution.py
+++ b/solution.py
@@ -99,7 +99,12 @@
     k = bias_part.shape[0] // 2
     wide = jnp.zeros((8, 2 * k), jnp.float32)
     wide = lax.dynamic_update_slice(wide, bias_part[None], (index // 2, 0))
-    small = lax.psum(jnp.concatenate([partial_gain_grad, wide.reshape(-1)]), DP_FSDP)
+
+    def process_the_threads(own_rows, net_axis):
+        far_arr = jnp.sum(lax.all_gather(own_rows, axis_name=net_axis), axis=0)
+        return far_arr
+
+    small = process_the_threads(jnp.concatenate([partial_gain_grad, wide.reshape(-1)]), DP_FSDP)
     gain_grad = small[:d]
     bias_grad = lax.dynamic_slice(small[d:], (index * k,), (k,))
     scaled_values = normed_rows_gradient * norm_gain_vector

time: 631 us -> 1480 us (2.35)
  the two profiles are of different devices: /device:TPU:2 before, /device:TPU:64 now
where the time goes in v1:
time: 1480 us
  waiting for transfers between devices  1390 us (94%)
  local copies, waits for them, and re-layouts  18.5 us (1%)
  matrix products  18.5 us (1%)
  starting transfers between devices  16.4 us (1%)
  other arithmetic  15 us (1%)
    all_gather x1, waiting for transfers between devices, process_the_threads(): far_arr = jnp.sum(lax.all_gather(own_rows, axis_name=net_axis), axis=0)  832 us
    reduce_scatter x1, waiting for transfers between devices, shards(): mine = lax.psum_scatter(mine, DP, scatter_dimension=0, tiled=True)  135 us
    all_gather x1, waiting for transfers between devices, shards(): whole = lax.all_gather(mine, DP, axis=0, tiled=True).astype(jnp.float32)  127 us
    reduce_scatter x1, waiting for transfers between devices, shards(): lax.psum_scatter(jnp.einsum('rk,dk->rd', pre_grad, up_weight, preferred_e...  97.9 us
    all_gather x1, waiting for transfers between devices, shards(): all_cot = lax.all_gather(packed_cot, ROWS_AXES, axis=0, tiled=True)  68.8 us
    all_gather x1, waiting for transfers between devices, shards(): lax.all_gather(normed_local, ROWS_AXES, axis=0, tiled=True)  66 us
  transfers between devices with their start and end apart: 10, of which 9 were waited for; matrix products, arithmetic and copies ran while one was open for 1% of the time, Pallas kernels for 0%

profile of v1, /device:TPU:64, one launch (start us, length us, event | category | flops | bytes accessed | tf_op | source)
XLA Modules:
  0.0 1478.0 jit_solution(10748626825134161292)
XLA Ops:
  7.2 0.8 fusion.26
  8.1 0.8 select_reduce_fusion
  9.0 0.7 compare_select_fusion
  9.9 1.2 convolution_convert_fusion.3
  11.1 1.0 all_to_all.8
  12.1 16.0 %all-to-all-start = ((bf16[32,4,2048]{2,1,0:T(4,128)(2,1)}), bf16[32,4,2048]{2,1,0:T(4,128)(2,1)S(1)}, u32[]{:S(2)}, u32[]{:S(2)}) async-start(bf16[32,4,2048]{2,1,0:T(4,128)(2,1)} %all_to_all.8), calls=%async_computation | async-start | bytes 1048576 | tf_op jit(solution)/shard_map/all_to_all | solution.py:18
  28.2 1.0 copy.16
  29.3 27.6 %all-to-all-done = bf16[32,4,2048]{2,1,0:T(4,128)(2,1)S(1)} async-done(((bf16[32,4,2048]{2,1,0:T(4,128)(2,1)}), bf16[32,4,2048]{2,1,0:T(4,128)(2,1)S(1)}, u32[]{:S(2)}, u32[]{:S(2)}) %all-to-all-start) | async-done | bytes 524320 | tf_op jit(solution)/shard_map/all_to_all | solution.py:18
  57.3 0.9 fusion.18
  58.4 0.7 slice.24
  59.7 1.8 all-gather.1
  61.5 66.0 %all-gather.13.cloned.1.call-done = bf16[1024,1024]{1,0:T(8,128)(2,1)} async-done(((bf16[128,1024]{1,0:T(8,128)(2,1)}), bf16[1024,1024]{1,0:T(8,128)(2,1)}) %all-gather.13.cloned.1.call-update) | async-done | bytes 2097168 | tf_op jit(solution)/shard_map/all_gather | solution.py:69
  127.5 4.5 fusion.33
  132.0 68.8 %all-gather.9.cloned.1.call-done = bf16[1024,1024]{1,0:T(8,128)(2,1)} async-done(((bf16[128,1024]{1,0:T(8,128)(2,1)}), bf16[1024,1024]{1,0:T(8,128)(2,1)}) %all-gather.9.cloned.1.call-update) | async-done | bytes 2097168 | tf_op jit(solution)/shard_map/all_gather | solution.py:68
  200.7 3.6 convolution_convert_fusion.1
  204.4 16.7 %all-gather.11.cloned.1.call-done = bf16[512,1024]{1,0:T(8,128)(2,1)} async-done(((bf16[256,1024]{1,0:T(8,128)(2,1)}), bf16[512,1024]{1,0:T(8,128)(2,1)}) %all-gather.11.cloned.1.call-update) | async-done | bytes 1048592 | tf_op jit(solution)/shard_map/all_gather | solution.py:51
  221.1 5.1 convert_reduce_fusion
  226.2 1.3 fusion.7
  227.5 1.5 pad_maximum_fusion
  229.1 21.8 %reduce-scatter.6.cloned.1.call-done = bf16[256,2048]{1,0:T(8,128)(2,1)} async-done(((bf16[512,2048]{1,0:T(8,128)(2,1)}), bf16[256,2048]{1,0:T(8,128)(2,1)}) %reduce-scatter.6.cloned.1.call-update) | async-done | bytes 1048592 | tf_op jit(solution)/shard_map/reduce_scatter | solution.py:84
  251.0 2.6 convolution_convert_fusion
  253.7 134.8 %reduce-scatter.8.cloned.1.call-done = bf16[8,2048]{1,0:T(8,128)(2,1)} async-done(((bf16[256,2048]{1,0:T(8,128)(2,1)}), bf16[8,2048]{1,0:T(8,128)(2,1)}) %reduce-scatter.8.cloned.1.call-update) | async-done | bytes 32784 | tf_op jit(solution)/shard_map/reduce_scatter | solution.py:85
  389.3 97.9 %reduce-scatter.4.cloned.1.call-done = bf16[128,1024]{1,0:T(8,128)(2,1)} async-done(((bf16[1024,1024]{1,0:T(8,128)(2,1)}), bf16[128,1024]{1,0:T(8,128)(2,1)}) %reduce-scatter.4.cloned.1.call-update) | async-done | bytes 262160 | tf_op jit(solution)/shard_map/reduce_scatter | solution.py:90
  487.2 1.2 fusion.25
  488.3 1.9 fusion.23
  490.3 127.4 %all-gather.17.cloned.1.call-done = bf16[256,2048]{1,0:T(8,128)(2,1)} async-done(((bf16[8,2048]{1,0:T(8,128)(2,1)}), bf16[256,2048]{1,0:T(8,128)(2,1)}) %all-gather.17.cloned.1.call-update) | async-done | bytes 1048592 | tf_op jit(solution)/shard_map/all_gather | solution.py:86
  617.6 1.5 convert_element_type.58
  619.2 1.3 copy.17
  620.5 1.1 slice.28
  621.6 832.3 %all-gather.19.cloned.1.call-done = f32[2621440]{0:T(1024)} async-done(((f32[5120]{0:T(1024)}), f32[2621440]{0:T(1024)}) %all-gather.19.cloned.1.call-update) | async-done | bytes 10485776 | tf_op jit(solution)/shard_map/all_gather | solution.py:104
  1453.9 11.8 reshape.52
  1465.7 4.5 reduce_sum.79
  (55 shorter events, 4.0 us)
Async XLA Ops:
  7.2 2.5 copy-start
  9.6 18.5 %copy-start.2 = (bf16[1024,256]{1,0:T(8,128)(2,1)S(1)}, bf16[1024,256]{1,0:T(8,128)(2,1)}, u32[]{:S(2)}) copy-start(bf16[1024,256]{1,0:T(8,128)(2,1)} %param.11) | copy-start | bytes 1572868
  12.1 45.3 %copy-start.3 = (f32[1024]{0:T(1024)S(1)}, f32[1024]{0:T(1024)}, u32[]{:S(2)}) copy-start(f32[1024]{0:T(1024)} %param.10) | copy-start | bytes 12292
  12.1 44.8 %all-to-all-start = ((bf16[32,4,2048]{2,1,0:T(4,128)(2,1)}), bf16[32,4,2048]{2,1,0:T(4,128)(2,1)S(1)}, u32[]{:S(2)}, u32[]{:S(2)}) async-start(bf16[32,4,2048]{2,1,0:T(4,128)(2,1)} %all_to_all.8), calls=%async_computation | async-start | bytes 1048576 | tf_op jit(solution)/shard_map/all_to_all | solution.py:18
  28.1 33.4 %all-gather.15.cloned.1.call-start = ((), (), s32[]{:S(2)}) async-start(), calls=%async_computation.7 | async-start | bytes 1572864 | tf_op jit(solution)/shard_map/all_gather | solution.py:50
  29.2 30.5 %copy-start.4 = (f32[256]{0:T(256)S(1)}, f32[256]{0:T(256)}, u32[]{:S(2)}) copy-start(f32[256]{0:T(256)} %param.12) | copy-start | bytes 3076
  29.2 98.3 %all-gather.13.cloned.1.call-start = ((), (), s32[]{:S(2)}) async-start(), calls=%async_computation.6 | async-start | bytes 2359296 | tf_op jit(solution)/shard_map/all_gather | solution.py:69
  58.3 142.4 %all-gather.9.cloned.1.call-start = ((), (), s32[]{:S(2)}) async-start(), calls=%async_computation.4 | async-start | bytes 2359296 | tf_op jit(solution)/shard_map/all_gather | solution.py:68
  59.1 162.0 %all-gather.11.cloned.1.call-start = ((), (), s32[]{:S(2)}) async-start(), calls=%async_computation.5 | async-start | bytes 1572864 | tf_op jit(solution)/shard_map/all_gather | solution.py:51
  59.7 191.2 %reduce-scatter.6.cloned.1.call-start = ((), (), s32[]{:S(2)}) async-start(), calls=%async_computation.9 | async-start | bytes 3145728 | tf_op jit(solution)/shard_map/reduce_scatter | solution.py:84
  204.3 21.9 %copy-start.6 = (bf16[1024,512]{0,1:T(8,128)(2,1)S(1)}, bf16[1024,512]{0,1:T(8,128)(2,1)}, u32[]{:S(2)}) copy-start(bf16[1024,512]{0,1:T(8,128)(2,1)} %all-gather.15.cloned.1.call-done) | copy-start | bytes 3145732
  221.1 5.1 copy-start.5
  226.2 1.3 copy-start.7
  229.1 21.9 %copy-start.8 = (bf16[1024,512]{1,0:T(8,128)(2,1)S(1)}, bf16[1024,512]{1,0:T(8,128)(2,1)}, u32[]{:S(2)}) copy-start(bf16[1024,512]{1,0:T(8,128)(2,1)} %copy-done.7) | copy-start | bytes 3145732
  229.1 159.4 %reduce-scatter.8.cloned.1.call-start = ((), (), s32[]{:S(2)}) async-start(), calls=%async_computation.10 | async-start | bytes 1081344 | tf_op jit(solution)/shard_map/reduce_scatter | solution.py:85
  250.9 236.2 %reduce-scatter.4.cloned.1.call-start = ((), (), s32[]{:S(2)}) async-start(), calls=%async_computation.8 | async-start | bytes 2359296 | tf_op jit(solution)/shard_map/reduce_scatter | solution.py:90
  253.6 364.0 %all-gather.17.cloned.1.call-start = ((), (), s32[]{:S(2)}) async-start(), calls=%async_computation.11 | async-start | bytes 1081344 | tf_op jit(solution)/shard_map/all_gather | solution.py:86
  388.5 1065.5 %all-gather.19.cloned.1.call-start = ((), (), s32[]{:S(2)}) async-start(), calls=%async_computation.12 | async-start | bytes 10506240 | tf_op jit(solution)/shard_map/all_gather | solution.py:104
  619.1 1.4 copy-start.1
Sparse Core Ops, SparseCore 0:
  31.6 20.2 all-gather.14
  58.4 69.0 all-gather.12
  131.3 69.3 all-gather.8
  202.7 18.3 all-gather.10
  229.2 21.6 reduce-scatter.5
  253.5 134.8 reduce-scatter.7
  393.1 94.0 reduce-scatter.3
  489.2 128.3 all-gather.16
  619.9 834.0 all-gather.18
